TPU v7x, 32 devices: a whole 2x2x4 slice. The times are simulated.
32 devices in a mesh: dp: 8 (over y, x, core), seq: 4 (over z).
Axes of the slice: x: 2, y: 2, z: 4, core: 2. Of those that a mesh axis runs over, the one named last changes fastest.
Arguments:
- tokens: bfloat16 [2, 8, 1024, 1024], P(None, 'dp', 'seq'), may hold values from -6 to 6
- segments: int32 [2, 8, 1024], P(None, 'dp'), may hold values from 0 to 3, never falling along the last dimension, each value on 1 to 800 neighbouring positions
- ln1_gain: float32 [1024], P(('dp', 'seq')), may hold values from 0.1 to 1.9
- in_weight: float32 [1024, 3072], P(('dp', 'seq')), may hold values from -0.1875 to 0.1875
- conv_kernel: float32 [3, 1024], P(None, ('dp', 'seq')), may hold values from -3 to 3
- out_weight: float32 [1024, 1024], P(('dp', 'seq')), may hold values from -0.1875 to 0.1875
- ln2_gain: float32 [1024], P(('dp', 'seq')), may hold values from 0.1 to 1.9
- gate_weight: float32 [1024, 4608], P(('dp', 'seq')), may hold values from -0.1875 to 0.1875
- up_weight: float32 [1024, 4608], P(('dp', 'seq')), may hold values from -0.1875 to 0.1875
- down_weight: float32 [4608, 1024], P(('dp', 'seq')), may hold values from -0.09375 to 0.09375
- cotangent: bfloat16 [2, 8, 1024, 1024], P(None, 'dp', 'seq'), may hold values from -6 to 6
Outputs:
- output: bfloat16 [2, 8, 1024, 1024], P(None, 'dp', 'seq')
- grad_tokens: bfloat16 [2, 8, 1024, 1024], P(None, 'dp', 'seq')
- grad_ln1: float32 [1024], P(('dp', 'seq'))
- grad_in: float32 [1024, 3072], P(('dp', 'seq'))
- grad_kernel: float32 [3, 1024], P(None, ('dp', 'seq'))
- grad_out: float32 [1024, 1024], P(('dp', 'seq'))
- grad_ln2: float32 [1024], P(('dp', 'seq'))
- grad_gate: float32 [1024, 4608], P(('dp', 'seq'))
- grad_up: float32 [1024, 4608], P(('dp', 'seq'))
- grad_down: float32 [4608, 1024], P(('dp', 'seq'))
Inputs may be any that keep to these rules, and one draw needn't show every extreme that they name: `segments`: along each sequence the document numbers start at 0 and never fall; equal numbers mark one document.
All inputs are finite; a program needn't handle non-finite values.
Results may differ from a plain program's by a relative error of at most 0.012.
The roundings to bfloat16 on the way count: a program that leaves them out, or rounds other values in their place, can miss the bound.
Values may be sent and summed in bfloat16 or wider, within the bound.
A program may use at most 192 MiB of HBM per device.

v0:
```python
import functools
import jax
import jax.numpy as jnp
from jax import lax
from jax.experimental import pallas as pl
from jax.experimental.pallas import tpu as pltpu
from jax.sharding import PartitionSpec as P

BF = jnp.bfloat16
F32 = jnp.float32
eps = 1e-05
MESH = pl.DeviceIdType.MESH
NN = (((1,), (0,)), ((), ()))
NT = (((1,), (1,)), ((), ()))
TN = (((0,), (0,)), ((), ()))
TP = 4
LANES = 128


def mm(left, right, dims):
    return lax.dot_general(left, right, dims, preferred_element_type=F32)


def when(pred, body):
    if pred is True:
        body()
    else:
        pl.when(pred)(body)


class Place:
    def __init__(self, nz):
        dp = lax.axis_index("dp")
        self.y = dp // TP
        self.i = dp % TP
        self.z = lax.axis_index("seq")
        self.nz = nz
        self.x = self.i // 2
        self.c = self.i % 2
        self.others = tuple(self._near(k) for k in range(nz - 1))

    def _near(self, k):
        ranks = [sorted((q for q in range(self.nz) if q != z), key=lambda q: abs(q - z)) for z in range(self.nz)]
        place = jnp.int32(ranks[0][k])
        for z in range(1, self.nz):
            place = jnp.where(self.z == z, ranks[z][k], place)
        return place

    def to_both_sides(self, cp, block, ssem, rsem):
        for to, there in ((self.z - 1, self.z > 0), (self.z + 1, self.z < self.nz - 1)):
            cp.send(block, block, ssem(to), rsem, self.at(z=to), there)

    def relay(self, cp, block, source, ssem, rsem):
        to = jnp.where(source < self.z, self.z + 1, self.z - 1)
        cp.send(block, block, ssem, rsem, self.at(z=to), (to >= 0) & (to < self.nz))

    def member(self, t):
        x = 1 - self.x if t // 2 else self.x
        c = 1 - self.c if t % 2 else self.c
        return x * 2 + c

    def at(self, y=None, i=None, z=None):
        y = self.y if y is None else y
        i = self.i if i is None else i
        z = self.z if z is None else z
        return (y * TP + i, z)


class Copies:
    def __init__(self):
        self.pending = []

    def send(self, src, dst, ssem, rsem, device, pred=True, group=None):
        def make():
            return pltpu.make_async_remote_copy(
                src_ref=src, dst_ref=dst, send_sem=ssem, recv_sem=rsem,
                device_id=device, device_id_type=MESH)
        when(pred, lambda: make().start())
        if group is None:
            self.pending.append((pred, make))

    def local(self, src, dst, sem):
        pltpu.make_async_copy(src, dst, sem).start()

    def arrived(self, ref, ssem, rsem, device, pred=True):
        when(pred, lambda: pltpu.make_async_remote_copy(
            src_ref=ref, dst_ref=ref, send_sem=ssem, recv_sem=rsem,
            device_id=device, device_id_type=MESH).wait_recv())

    def drain(self, count=None):
        done = self.pending[:count]
        self.pending = self.pending[len(done):]
        for pred, make in done:
            when(pred, lambda make=make: make().wait_send())


def entry_barrier(p):
    bar = pltpu.get_barrier_semaphore()
    there = [p.at(i=p.member(t)) for t in range(1, TP)] + [p.at(y=1 - p.y)] + [p.at(z=q) for q in p.others]
    for device in there:
        pl.semaphore_signal(bar, inc=1, device_id=device, device_id_type=MESH)
    pl.semaphore_wait(bar, len(there))


def gather_pieces(width):
    half = width // 2
    return (
        (4, 0, LANES, "zyx"),
        (0, 0, half, "zyx"), (0, half, half, "zxy"),
        (2, 0, half, "xzy"), (2, half, half, "yzx"),
        (1, 0, half, "zyx"), (1, half, half, "zxy"),
        (3, 0, half, "xzy"), (3, half, half, "yzx"),
    )


def sum_pieces(width):
    half = width // 2
    return (
        (3, 0, half, "zyx"), (3, half, half, "zxy"),
        (1, 0, half, "zyx"), (1, half, half, "zxy"),
        (0, 0, half, "zyx"), (0, half, half, "zxy"),
        (2, 0, half, "zyx"), (2, half, half, "zxy"),
        (4, 0, LANES, "zyx"),
    )


def gather_sems(nz, count):
    D = pltpu.SemaphoreType.DMA
    return [D((count, 2, 2 * nz)), D((count, 2, nz)), D((count, nz)), D((count, nz)), D((count, 2, nz)),
            D((count, 2, nz)), D((count,)), D((count,))]


def gather_flow(p, cp, n, piece, W, sems):
    s_z, r_z, s_1, r_1, s_2, r_2, s_c, r_c = sems
    _, c0, cn, order = piece
    cs = slice(c0, c0 + cn)
    z, nz = p.z, p.nz
    a_is_x = order.index("x") < order.index("y")
    zfirst = order[0] == "z"

    def blk(a, b, zz):
        y, x = (b, a) if a_is_x else (a, b)
        return W.at[y, x, p.c, zz, :, cs]
    a, b = (p.x, p.y) if a_is_x else (p.y, p.x)
    dev_x, dev_y = p.at(i=p.member(2)), p.at(y=1 - p.y)
    dev_a, dev_b = (dev_x, dev_y) if a_is_x else (dev_y, dev_x)

    def core(aa, bb, zz):
        r = blk(aa, bb, zz)
        cp.send(r, r, s_c.at[n], r_c.at[n], p.at(i=p.member(1)), group=True)

    def zsend(aa):
        p.to_both_sides(cp, blk(aa, b, z), lambda to: s_z.at[n, aa, to], r_z.at[n, aa, z])

    def asend(zz):
        r = blk(a, b, zz)
        cp.send(r, r, s_1.at[n, zz], r_1.at[n, zz], dev_a)

    def bsend(aa, zz):
        r = blk(aa, b, zz)
        cp.send(r, r, s_2.at[n, aa, zz], r_2.at[n, aa, zz], dev_b)

    asend(z)
    zsend(a)
    bsend(a, z)
    core(a, b, z)
    yield "first"
    if not zfirst:
        cp.arrived(blk(1 - a, b, z), s_1.at[n, z], r_1.at[n, z], p.at())
        zsend(1 - a)
        bsend(1 - a, z)
        core(1 - a, b, z)
    for zz in p.others:
        yield "z"
        for aa in ((a,) if zfirst else (a, 1 - a)):
            cp.arrived(blk(aa, b, zz), s_z.at[n, aa, zz], r_z.at[n, aa, zz], p.at())
            p.relay(cp, blk(aa, b, zz), zz, s_z.at[n, aa, nz + zz], r_z.at[n, aa, zz])
            if zfirst:
                asend(zz)
            bsend(aa, zz)
            core(aa, b, zz)
    if zfirst:
        yield "second"
        for zz in (z,) + p.others:
            cp.arrived(blk(1 - a, b, zz), s_1.at[n, zz], r_1.at[n, zz], p.at())
            bsend(1 - a, zz)
            core(1 - a, b, zz)
    for zz in (z,) + p.others:
        yield "last axis"
        for aa in (a, 1 - a):
            cp.arrived(blk(aa, 1 - b, zz), s_2.at[n, aa, zz], r_2.at[n, aa, zz], p.at())
            core(aa, 1 - b, zz)
    yield "core"
    cp.arrived(W.at[:, :, 1 - p.c, :, :, cs], s_c.at[n], r_c.at[n], p.at())
    cp.pending.append((True, lambda: pltpu.make_async_remote_copy(
        src_ref=W.at[:, :, p.c, :, :, cs], dst_ref=W.at[:, :, p.c, :, :, cs], send_sem=s_c.at[n],
        recv_sem=r_c.at[n], device_id=p.at(i=p.member(1)), device_id_type=MESH)))


def sum_sems(nz, count):
    D = pltpu.SemaphoreType.DMA
    return [D((count,)), D((count,)), D((count, nz)), D((count, nz)), D((count, nz)), D((count, nz)),
            D((count, nz)), D((count, nz))]


def sum_scratch(nz, shard, pieces):
    return dict(
        one=[pltpu.VMEM((2, nz, shard, q[2]), BF) for q in pieces],
        two=[pltpu.VMEM((nz if q[3][0] == "z" else 1, shard, q[2]), BF) for q in pieces],
        path=[pltpu.VMEM((nz, 1 if q[3][0] == "z" else 2, shard, q[2]), BF) for q in pieces],
    )


def sum_flow(p, cp, n, piece, G, LC, L1, L2, LZ, out, sems):
    s_c, r_c, s_1, r_1, s_2, r_2, s_z, r_z = sems
    _, c0, cn, order = piece
    cs = slice(c0, c0 + cn)
    z = p.z
    targets = p.others[::-1] + (z,)
    zlast = order[0] == "z"
    b_is_y = order.index("x") < order.index("y")
    b, a = (p.y, p.x) if b_is_y else (p.x, p.y)
    dev_x, dev_y = p.at(i=p.member(2)), p.at(y=1 - p.y)
    dev_b, dev_a = (dev_y, dev_x) if b_is_y else (dev_x, dev_y)

    def g(bb, aa, zz):
        y, x = (bb, aa) if b_is_y else (aa, bb)
        return (y, x, p.c, zz, slice(None), cs)

    def f(v):
        return v.astype(F32)

    def lc(bb, aa, zz):
        y, x = (bb, aa) if b_is_y else (aa, bb)
        return (y, x, zz)

    def row(bb, zz, aa=None):
        aa = slice(None) if aa is None else pl.ds(aa, 1)
        y, x = (bb, aa) if b_is_y else (aa, bb)
        return G.at[y, x, p.c, zz, :, cs]
    cp.send(G.at[:, :, 1 - p.c, :, :, cs], LC, s_c.at[n], r_c.at[n], p.at(i=p.member(1)))
    LZ[z] = jnp.zeros(LZ.shape[1:], BF)
    yield
    cp.arrived(LC, s_c.at[n], r_c.at[n], p.at())
    for zz in targets:
        for aa in range(2):
            i = g(1 - b, aa, zz)
            G[i] = (f(G[i]) + f(LC[lc(1 - b, aa, zz)])).astype(BF)
        cp.send(row(1 - b, zz), L1.at[:, zz], s_1.at[n, zz], r_1.at[n, zz], dev_b)
    for zz in targets:
        for aa in range(2):
            i = g(b, aa, zz)
            G[i] = (f(G[i]) + f(LC[lc(b, aa, zz)])).astype(BF)
    if zlast:
        yield
        for zz in targets:
            cp.arrived(L1.at[:, zz], s_1.at[n, zz], r_1.at[n, zz], p.at())
            i = g(b, 1 - a, zz)
            G[i] = (f(G[i]) + f(L1[1 - a, zz])).astype(BF)
            cp.send(G.at[i], L2.at[zz], s_2.at[n, zz], r_2.at[n, zz], dev_a)

    def own(zz, k):
        if zlast:
            return f(G[g(b, a, zz)]) + f(L1[a, zz]) + f(L2[zz])
        return f(G[g(b, k, zz)]) + f(L1[k, zz])
    yield
    for zz in targets:
        if zlast:
            cp.arrived(L2.at[zz], s_2.at[n, zz], r_2.at[n, zz], p.at())
        else:
            cp.arrived(L1.at[:, zz], s_1.at[n, zz], r_1.at[n, zz], p.at())
        if zz is z:
            continue
        for k in range(1 if zlast else 2):
            G[g(b, a if zlast else k, zz)] = own(zz, k).astype(BF)
        cp.send(row(b, zz, a if zlast else None), LZ.at[z], s_z.at[n, zz], r_z.at[n, z], p.at(z=zz))
    yield
    for zz in p.others:
        cp.arrived(LZ.at[zz], s_z.at[n, zz], r_z.at[n, zz], p.at())

    def total(k):
        v = own(z, k)
        for zz in range(p.nz):
            v = v + f(LZ[zz, k])
        return v
    if zlast:
        out[:, cs] = total(0)
        return
    G[g(b, 1 - a, z)] = total(1 - a).astype(BF)
    cp.send(G.at[g(b, 1 - a, z)], L2.at[0], s_2.at[n, 0], r_2.at[n, 0], dev_a)
    out[:, cs] = total(a)
    yield
    cp.arrived(L2.at[0], s_2.at[n, 0], r_2.at[n, 0], p.at())
    out[:, cs] += f(L2[0])


def slot(ref, t):
    return ref.at[t // 2, t % 2]


def block_body(parts, nz, x_in, df_in, masks, b0, b1, b2, b3, b4, gus, ds,
               out_o, gx_o, ogu_o, od_o, m012, m3, m4, W0, W1, W2, W3, W4, SV32, SV16, s):
    p = Place(nz)
    z = p.z
    rows, width = x_in.shape
    shard = gus.shape[2]
    npos = 2 * nz
    count = rows // 2
    half = width // 2
    low = rows // (2 * nz)
    offs = [sum(parts[:k]) for k in range(len(parts))]
    CH = [(offs[k] * npos, parts[k] * npos) for k in range(len(parts))]
    K = len(parts)
    cp, cx, ct = Copies(), Copies(), Copies()
    cg = [Copies() for _ in range(K)]
    first, last = z == 0, z == nz - 1
    inner_l, inner_r = z > 0, z < nz - 1
    H, dF, WGU, WD, dHa, Zb, dAb, dGb = (s[k] for k in ("H", "dF", "WGU", "WD", "dHa", "Zb", "dAb", "dGb"))
    GGU = WGU
    GD, RY, ZGU, ZD, YD, LX, SX = (s[k] for k in ("GD", "RY", "ZGU", "ZD", "YD", "LX", "SX"))
    sem_h, s_p0, r_p0, s_z, r_z, s_y, r_y, s_dz, r_dz, s_dy, r_dy = (
        s[k] for k in ("sem_h", "s_p0", "r_p0", "s_z", "r_z", "s_y", "r_y", "s_dz", "r_dz", "s_dy", "r_dy"))
    s_gy, r_gy, s_gz, r_gz, s_gt, r_gt, s_ez, r_ez, s_ey, r_ey, s_x, r_x = (
        s[k] for k in ("s_gy", "r_gy", "s_gz", "r_gz", "s_gt", "r_gt", "s_ez", "r_ez", "s_ey", "r_ey", "s_x", "r_x"))
    sem = s["sem"]
    GN, SG, SM, PV, NX = (s[k] for k in ("GN", "SG", "SM", "PV", "NX"))
    GS = SM
    W = (W0, W1, W2, W3, W4)
    sums = tuple(m012.at[:, q * width:(q + 1) * width] for q in range(3)) + (m3, m4)

    def cols(k):
        return slice(CH[k][0], CH[k][0] + CH[k][1])

    def rws(k):
        return slice(offs[k], offs[k] + parts[k])

    class Load:
        def __init__(self, n, *pairs):
            self.copies = [pltpu.make_async_copy(a, b, sem.at[n + k]) for k, (a, b) in enumerate(pairs)]

        def start(self):
            for c in self.copies:
                c.start()
            return self

        def wait(self):
            for c in self.copies:
                c.wait()

    own_w = Load(0, *[(b, w.at[p.y, p.x, p.c, z]) for b, w in zip((b0, b1, b2, b3, b4), W)]).start()
    own_x = Load(5, (x_in, SX.at[0])).start()
    df_blocks = df_in
    own_df = Load(6, (df_blocks, slot(dF, 0))).start()
    own_gu = Load(7, (gus.at[p.i], WGU.at[p.y, p.i, z])).start()
    own_d = Load(8, *[(ds.at[rws(k)], WD[k].at[p.y, z]) for k in range(K)]).start()
    entry_barrier(p)

    ZGU[z] = jnp.zeros(ZGU.shape[1:], BF)
    for k in range(K):
        ZD[k][z] = jnp.zeros(ZD[k].shape[1:], BF)

    @pl.when(first)
    def _():
        PV[...] = jnp.zeros(PV.shape, BF)

    @pl.when(last)
    def _():
        NX[...] = jnp.zeros(NX.shape, BF)

    def p0(k):
        for t in (2, 3, 1):
            m = p.member(t)
            cg[k].send(gus.at[m, :, :, cols(k)], WGU.at[p.y, p.i, z, :, :, cols(k)],
                       s_p0.at[k, t - 1], r_p0.at[k, t - 1], p.at(i=m))

    def acts(dst, q):
        for t in (2, 1):
            cp.send(slot(dst, 0), slot(dst, t), sem_h.at[q, 0, t - 1], sem_h.at[q, 1, t - 1], p.at(i=p.member(t)))

    def acts_wait(dst, q, t):
        cp.arrived(slot(dst, t), sem_h.at[q, 0, t - 1], sem_h.at[q, 1, t - 1], p.at(i=p.member(t)))

    def acts_forward(dst, q):
        acts_wait(dst, q, 2)
        cp.send(slot(dst, 2), slot(dst, 3), sem_h.at[q, 0, 2], sem_h.at[q, 1, 2], p.at(i=p.member(1)))

    def gu_blk(k, y, zz):
        return WGU.at[y, :, zz, :, :, cols(k)]

    def ysend(k, zz):
        b = gu_blk(k, p.y, zz)
        cg[k].send(b, b, s_y.at[k, zz], r_y.at[k, zz], p.at(y=1 - p.y))

    def flow_ag(k):
        W = WD[k]
        for t in (1, 2, 3):
            m = p.member(t)
            cp.arrived(WGU.at[p.y, m, z, :, :, cols(k)], s_p0.at[k, t - 1], r_p0.at[k, t - 1], p.at(i=m))
        p.to_both_sides(cg[k], gu_blk(k, p.y, z), lambda to: s_z.at[k, to], r_z.at[k, z])
        b = W.at[p.y, z]
        cg[k].send(b, b, s_dy.at[k], r_dy.at[k], p.at(y=1 - p.y))
        p.to_both_sides(cg[k], b, lambda to: s_dz.at[k, p.y, to], r_dz.at[k, p.y, z])
        yield
        ysend(k, z)
        b = W.at[1 - p.y, z]
        cp.arrived(b, s_dy.at[k], r_dy.at[k], p.at())
        p.to_both_sides(cg[k], b, lambda to: s_dz.at[k, 1 - p.y, to], r_dz.at[k, 1 - p.y, z])
        for zz in p.others:
            yield
            b = gu_blk(k, p.y, zz)
            cp.arrived(b, s_z.at[k, zz], r_z.at[k, zz], p.at())
            p.relay(cg[k], b, zz, s_z.at[k, nz + zz], r_z.at[k, zz])
            ysend(k, zz)
            for y in (p.y, 1 - p.y):
                b = W.at[y, zz]
                cp.arrived(b, s_dz.at[k, y, zz], r_dz.at[k, y, zz], p.at())
                p.relay(cg[k], b, zz, s_dz.at[k, y, nz + zz], r_dz.at[k, y, zz])
        yield
        for zz in (z,) + p.others:
            cp.arrived(gu_blk(k, 1 - p.y, zz), s_y.at[k, zz], r_y.at[k, zz], p.at())

    targets = p.others[::-1] + (z,)

    def flow_rs_gu(k, w):
        c = cols(k)
        for zz in targets:
            cp.send(GGU.at[1 - p.y, :, zz, w, :, c], RY.at[:, zz, w, :, c],
                    s_gy.at[k, w, zz], r_gy.at[k, w, zz], p.at(y=1 - p.y))
        for zz in p.others[::-1]:
            yield
            cp.arrived(RY.at[:, zz, w, :, c], s_gy.at[k, w, zz], r_gy.at[k, w, zz], p.at())
            for j in range(TP):
                GGU[p.y, j, zz, w, :, c] = (
                    GGU[p.y, j, zz, w, :, c].astype(F32) + RY[j, zz, w, :, c].astype(F32)).astype(BF)
            cp.send(GGU.at[p.y, :, zz, w, :, c], ZGU.at[z, :, w, :, c], s_gz.at[k, w, zz], r_gz.at[k, w, z],
                    p.at(z=zz))
        yield
        cp.arrived(RY.at[:, z, w, :, c], s_gy.at[k, w, z], r_gy.at[k, w, z], p.at())
        for zz in p.others:
            cp.arrived(ZGU.at[zz, :, w, :, c], s_gz.at[k, w, zz], r_gz.at[k, w, zz], p.at())
        for j in range(TP):
            v = GGU[p.y, j, z, w, :, c].astype(F32) + RY[j, z, w, :, c].astype(F32)
            for zz in range(nz):
                v = v + ZGU[zz, j, w, :, c].astype(F32)
            GGU[p.y, j, z, w, :, c] = v.astype(BF)
        for t in (2, 3, 1):
            m = p.member(t)
            cp.send(GGU.at[p.y, m, z, w, :, c], ogu_o.at[p.i, w, :, c], s_gt.at[k, w, t - 1], r_gt.at[k, w, t - 1],
                    p.at(i=m))
        own_out.append(Load(11 + 2 * k + w, (GGU.at[p.y, p.i, z, w, :, c], ogu_o.at[p.i, w, :, c])).start())
        yield
        for t in (1, 2, 3):
            m = p.member(t)
            cp.arrived(ogu_o.at[m, w, :, c], s_gt.at[k, w, t - 1], r_gt.at[k, w, t - 1], p.at(i=m))

    def flow_rs_d(k):
        G, L, Y = GD[k], ZD[k], YD[k]
        for zz in targets:
            cp.send(G.at[1 - p.y, zz], Y.at[zz], s_ey.at[k, zz], r_ey.at[k, zz], p.at(y=1 - p.y))
        for zz in p.others[::-1]:
            yield
            cp.arrived(Y.at[zz], s_ey.at[k, zz], r_ey.at[k, zz], p.at())
            G[p.y, zz] = (G[p.y, zz].astype(F32) + Y[zz].astype(F32)).astype(BF)
            cp.send(G.at[p.y, zz], L.at[z], s_ez.at[k, zz], r_ez.at[k, z], p.at(z=zz))
        yield
        cp.arrived(Y.at[z], s_ey.at[k, z], r_ey.at[k, z], p.at())
        for zz in p.others:
            cp.arrived(L.at[zz], s_ez.at[k, zz], r_ez.at[k, zz], p.at())
        v = G[p.y, z].astype(F32) + Y[z].astype(F32)
        for zz in range(nz):
            v = v + L[zz].astype(F32)
        od_o[rws(k), :] = v

    live, own_out = [], []

    def pump(n=1, which=None):
        for _ in range(n):
            for f in list(live if which is None else which):
                if f in live and next(f, "end") == "end":
                    live.remove(f)

    def run(*gens):
        for g in gens:
            for _ in g:
                pass
            if g in live:
                live.remove(g)

    own_w.wait()
    gp = gather_pieces(width)
    gather = [gather_flow(p, cp, n, q, W[q[0]], s["gather"]) for n, q in enumerate(gp)]
    states = {}

    def gather_to(*stops):
        left = list(gather)
        while left:
            for f in list(left):
                if states.get(f) in stops:
                    left.remove(f)
                else:
                    states[f] = next(f)
    gather_to("first")
    own_gu.wait()
    own_d.wait()
    own_df.wait()
    gather_to("z")
    for k in range(K):
        p0(k)
    gather_to("last axis")
    acts(dF, 1)
    ag = [flow_ag(k) for k in range(K)]
    for g in ag:
        next(g)
    for g in ag:
        next(g)
    gather_to("core")

    def need(*panels):
        for f, q in zip(gather, gp):
            if q[0] in panels:
                next(f, None)

    def panel(q, buf, n):
        return Load(n, *[(W[q].at[:, :, :, :, :, h * half:(h + 1) * half], buf.at[:, h, :, :, :, :, pl.ds(0, half)]) for h in range(2)])

    def half_panel(buf, h):
        return buf[:, h, :, :, :, :, :half].reshape(width, half)

    need(4)
    Load(20, (W4, SM)).start().wait()
    GN[...] = SM[...].reshape(width, LANES).astype(F32).T[:8]
    need(0)
    wb = panel(0, dAb, 21).start()
    own_x.wait()

    def norm(v):
        inv = lax.rsqrt(jnp.mean(v * v, axis=-1, keepdims=True) + eps)
        return inv, v * inv

    def tiles(size):
        return [slice(t * size, (t + 1) * size) for t in range(rows // size)]

    def norm_one(m, _):
        rs = pl.ds(pl.multiple_of(m * 128, 128), 128)
        _, n1 = norm(SX[0, rs].astype(F32))
        SX[1, rs] = (n1 * GN[0:1]).astype(BF)
        return 0
    lax.fori_loop(0, rows // 128, norm_one, 0)
    save_h1 = Load(30, (SX.at[1], SV16.at[0])).start()

    def project(buf, dst):
        for h in range(2):
            dHa[dst, :, h * half:(h + 1) * half] = mm(SX[1], half_panel(buf, h), NN)
    need(2)
    wu = panel(2, dGb, 23).start()
    wb.wait()
    project(dAb, 0)
    need(1)
    wc = panel(1, dAb, 21).start()
    wu.wait()
    project(dGb, 2)
    save_bu = Load(31, (dHa.at[0], SV32.at[0]), (dHa.at[2], SV32.at[2])).start()

    def make_bx(m, _):
        rs = pl.ds(pl.multiple_of(m * 128, 128), 128)
        SX[2, rs] = (dHa[0, rs] * dHa[2, rs]).astype(BF)
        return 0
    lax.fori_loop(0, rows // 128, make_bx, 0)
    s_h, r_h = s["s_h"], s["r_h"]
    for m in range(2):
        cp.send(SX.at[2, pl.ds((m + 1) * count - 16, 16)], PV.at[m], s_h.at[0, m], r_h.at[0, m],
                p.at(z=z + 1), inner_r)
    save_bx = Load(33, (SX.at[2], SV16.at[1])).start()
    live.extend(ag)
    pump(1, ag[:1])
    need(3)
    wo = panel(3, dGb, 23).start()
    wc.wait()
    project(dAb, 1)
    save_c = Load(34, (dHa.at[1], SV32.at[1])).start()
    for m in range(2):
        cp.arrived(PV.at[m], s_h.at[0, m], r_h.at[0, m], p.at(), inner_l)

    def earlier(v, prev, back):
        r = lax.broadcasted_iota(jnp.int32, v.shape, 0)
        n = prev.shape[0]
        moved = pltpu.roll(v, back, 0)
        moved = jnp.where(r == back - 1, prev[n - 1:n], moved)
        return jnp.where(r == 0, prev[n - back:n - back + 1], moved)

    def later(v, after, ahead):
        r = lax.broadcasted_iota(jnp.int32, v.shape, 0)
        n = v.shape[0]
        moved = pltpu.roll(v, n - ahead, 0)
        moved = jnp.where(r == n - ahead, after[0:1], moved)
        return jnp.where(r == n - 1, after[ahead - 1:ahead], moved)

    lanes = 256
    nl = width // lanes

    def conv(q, _):
        m, c = q // nl, q % nl
        ls = pl.ds(pl.multiple_of(c * lanes, lanes), lanes)
        rs = pl.ds(pl.multiple_of(m * count, count), count)
        v = SX[2, rs, ls].astype(F32)
        prev = PV[m, :, ls].astype(F32)
        mk = masks[m]
        total = GN[2:3, ls] * earlier(v, prev, 2) * mk[:count, 0:1]
        total = total + GN[3:4, ls] * earlier(v, prev, 1) * mk[:count, 1:2]
        total = total + GN[4:5, ls] * v * mk[:count, 2:3]
        dHa[3, rs, ls] = total
        LX[0, rs, ls] = (dHa[1, rs, ls] * total).astype(BF)
        return 0
    lax.fori_loop(0, 2 * nl, conv, 0)
    save_cv = Load(35, (dHa.at[3], SV32.at[3]), (LX.at[0], SV16.at[2])).start()
    save_bu.wait()
    pump(1, ag)
    wo.wait()
    for h in range(2):
        hs = slice(h * half, (h + 1) * half)
        dHa[0, :, hs] = SX[0, :, hs].astype(F32) + mm(LX[0], half_panel(dGb, h), NN)

    def norm_two(m, _):
        rs = pl.ds(pl.multiple_of(m * nz * shard, nz * shard), nz * shard)
        _, n2 = norm(dHa[0, rs])
        H[0, 0, m // 2, m % 2] = (n2 * GN[1:2]).astype(BF).reshape(nz, shard, width)
        return 0
    lax.fori_loop(0, 4, norm_two, 0)
    save_r = Load(37, (dHa.at[0], SV32.at[4])).start()
    save_cv.wait()
    acts(H, 0)
    save_h1.wait()
    save_bx.wait()
    save_c.wait()
    save_r.wait()
    pump(1, ag)

    def half_blocks(v):
        return v.reshape(2, nz, shard, v.shape[-1])

    def fwd_mid(k, t):
        c0, cn = CH[k]
        c = cols(k)
        wg = WGU[:, :, :, 0, :, c].reshape(width, cn)
        wu = WGU[:, :, :, 1, :, c].reshape(width, cn)
        wd = WD[k][...].reshape(cn, width)

        def some(r, _):
            rs = pl.ds(pl.multiple_of(r * count, count), count)
            h = H[t // 2, t % 2, r].reshape(count, width)
            a = mm(h, wg, NN)
            g = mm(h, wu, NN)
            dz = mm(dF[t // 2, t % 2, r].reshape(count, width), wd, NT)
            sg = 1.0 / (1.0 + jnp.exp(-a))
            act = a * sg
            Zb[t, r, :, :, :, c] = half_blocks((act * g).astype(BF))
            da = (dz * g * sg * (1.0 + a * (1.0 - sg))).astype(BF)
            dg = (dz * act).astype(BF)
            dAb[t // 2, t % 2, r, :, :, :, :cn] = half_blocks(da)
            dGb[t // 2, t % 2, r, :, :, :, :cn] = half_blocks(dg)
            d = mm(da, wg, NT) + mm(dg, wu, NT)
            if k == 0:
                dHa[t, rs] = d
            else:
                dHa[t, rs] += d
            return 0
        lax.fori_loop(0, 2, some, 0)

    def ffn_out(t, put):
        def some(r, _):
            f = None
            for k in range(K):
                v = mm(Zb[t, r, :, :, :, cols(k)].reshape(count, CH[k][1]), WD[k][...].reshape(CH[k][1], width), NN)
                f = v if f is None else f + v
            put(pl.ds(pl.multiple_of(r * count, count), count), f)
            return 0
        lax.fori_loop(0, 2, some, 0)

    tok = TP * rows

    def grads(k):
        c0, cn = CH[k]
        c = cols(k)
        for w, src in ((0, dAb), (1, dGb)):
            def body(m, _, w=w, src=src):
                y, j = m // 2, (m % 2) * 2
                f = 2 * nz * shard
                ms = pl.ds(pl.multiple_of(m * f, f), f)
                v = mm(H[:, :, :, :, :, :, ms].reshape(tok, f), src[:, :, :, :, :, :, :cn].reshape(tok, cn), TN)
                GGU[y, pl.ds(j, 2), :, w, :, c] = v.astype(BF).reshape(2, nz, shard, cn)
                return 0
            lax.fori_loop(0, TP, body, 0)
            begin((k, w), flow_rs_gu(k, w))
            if k == K - 1:
                advance(*(((0, 0), (0, 1)) if w == 0 else ((0, 0), (0, 1), (0, 2))))
        r = parts[k]
        for b in range(cn // 128):
            zb = Zb[:, :, :, :, :, c0 + b * 128:c0 + (b + 1) * 128].reshape(tok, 128)
            v = mm(zb, dF[...].reshape(tok, width), TN).astype(BF)
            lo = b * 128
            while lo < (b + 1) * 128:
                pos, q = lo // r, lo % r
                n = min(r - q, (b + 1) * 128 - lo)
                GD[k][pos // nz, pos % nz, q:q + n] = v[lo - b * 128:lo - b * 128 + n]
                lo += n
        begin((k, 2), flow_rs_d(k))

    rs_flows = {}

    def begin(key, flow):
        next(flow)
        rs_flows[key] = flow
        live.append(flow)

    def advance(*keys):
        for key in keys:
            if rs_flows[key] in live:
                pump(1, [rs_flows[key]])

    def x_land(q, e):
        return LX.at[2 + q] if e == 2 else LX.at[e]

    def x_send1(q, e, value=None):
        if value is not None:
            SX[e] = value.astype(BF)
        cx.send(SX.at[e], x_land(q, e), s_x.at[q, e], r_x.at[q, e], p.at(i=p.member(1)))

    def x_wait(q, e):
        cx.arrived(x_land(q, e), s_x.at[q, e], r_x.at[q, e], p.at(i=p.member(2 if e == 2 else 1)))

    def x_send2(q, acc):
        x_wait(q, 1)
        SX[2] = (acc[...] + LX[1].astype(F32)).astype(BF)
        cx.send(SX.at[2], x_land(q, 2), s_x.at[q, 2], r_x.at[q, 2], p.at(i=p.member(2)))

    def x_add(q, acc, e):
        x_wait(q, e)
        acc[...] += x_land(q, e)[...].astype(F32)

    acts_forward(dF, 1)
    before = 0
    for k in range(K):
        run(ag[k])
        if k == K - 1:
            cp.drain(before)
        if k == 0:
            acts_wait(H, 0, 1)
            acts_wait(dF, 1, 1)
            fwd_mid(0, 0)
            fwd_mid(0, 1)
            acts_forward(H, 0)
            acts_wait(dF, 1, 3)
            fwd_mid(0, 2)
            acts_wait(H, 0, 3)
            fwd_mid(0, 3)
            pump(1, ag[1:2])
        else:
            for t in (3, 2, 1, 0):
                fwd_mid(k, t)
                if k == K - 1 and t == 3:
                    x_send1(0, 1, dHa[3])
                if k == K - 1 and t == 2:
                    x_send2(0, dHa.at[2])
                if k == K - 1 and t == 1:
                    x_send1(0, 0, dHa[1])
                if k == 1:
                    advance(*{3: (), 2: ((0, 0),), 1: ((0, 0),), 0: ((0, 0), (0, 1))}[t])
        cg[k].drain()
        before = len(cp.pending)
        grads(k)
    wo = panel(3, dAb, 21).start()
    x_add(0, dHa.at[0], 0)
    pl.semaphore_signal(s["ready"], inc=1, device_id=p.at(i=p.member(1)), device_id_type=MESH)
    pr = Load(40, (SV32.at[4], dHa.at[2])).start()
    advance((0, 1), (0, 2), (0, 2))

    def keep(n):
        def put(rs, v):
            dHa[n, rs] = v
        return put

    def stage(e):
        def put(rs, v):
            SX[e, rs] = v.astype(BF)
        return put
    ffn_out(2, keep(1))
    ffn_out(0, keep(3))
    advance((0, 1), (0, 2), (1, 0))
    cx.drain(1)
    cx.pending.append(cx.pending.pop(0))
    cx.drain(1)
    ffn_out(1, stage(0))
    ffn_out(3, stage(1))
    pl.semaphore_wait(s["ready"], 1)
    x_send1(1, 0)
    x_send1(1, 1)
    advance((1, 0))
    x_add(0, dHa.at[0], 2)
    cx.drain(1)
    x_send2(1, dHa.at[1])
    x_add(1, dHa.at[3], 0)

    pc = Load(41, (SV32.at[1], dHa.at[1])).start()
    cx.drain(2)
    py = Load(42, (SV16.at[2], SX.at[0]), (SV16.at[0], SX.at[1])).start()
    pr.wait()
    SG[...] = jnp.zeros(SG.shape, F32)

    def back_two(m, _):
        n = nz * shard
        rs = pl.ds(pl.multiple_of(m * n, n), n)
        r = dHa[2, rs]
        dHa[3, rs] += r
        inv, n2 = norm(r)
        d = dHa[0, rs]
        SG[1:2] += jnp.sum(d * n2, axis=0, keepdims=True)
        dn = d * GN[1:2]
        df = dF[0, 0, m // 2, m % 2].reshape(n, width).astype(F32)
        dr = df + inv * (dn - n2 * jnp.mean(dn * n2, axis=-1, keepdims=True))
        dHa[0, rs] = dr
        WD[0][m // 2, pl.ds((m % 2) * (nz // 2), nz // 2), :low] = dr.astype(BF).reshape(nz // 2, low, width)
        return 0
    lax.fori_loop(0, 4, back_two, 0)
    pcv = Load(44, (SV32.at[3], dHa.at[2])).start()
    advance((1, 0), (1, 1))
    wo.wait()
    pc.wait()
    pcv.wait()
    wbk = panel(0, dGb, 23).start()

    def back_y(m, _):
        rs = pl.ds(pl.multiple_of(m * count, count), count)
        do = WD[0][m, :, :low].reshape(count, width)
        dy = mm(do[:, :half], half_panel(dAb, 0), NT) + mm(do[:, half:], half_panel(dAb, 1), NT)
        LX[1, rs] = (dy * dHa[2, rs]).astype(BF)
        WD[1][m, :, :low] = (dy * dHa[1, rs]).astype(BF).reshape(nz, low, width)
        return 0
    lax.fori_loop(0, 2, back_y, 0)
    advance((1, 0), (1, 1))
    wck = panel(1, dAb, 21).start()
    for m in range(2):
        cp.send(WD[1].at[m, 0, pl.ds(0, 16)], NX.at[m], s_h.at[1, m], r_h.at[1, m], p.at(z=z - 1), inner_l)
    pu = Load(41, (SV32.at[2], dHa.at[1])).start()
    pb = Load(44, (SV32.at[0], dHa.at[2])).start()

    panels = (H.at[0], H.at[1], dF.at[0], dF.at[1], GS)
    sp = sum_pieces(width)

    mix = {}

    def start_sums(q):
        for n, piece in enumerate(sp):
            if piece[0] != q:
                continue
            _, c0, cn, _ = piece
            lc = Zb.at[q, :, :, :, :, pl.ds(c0, cn)] if q < 4 else Zb.at[3, :, :, :, :, pl.ds(width, LANES)]
            g = sum_flow(p, ct, n, piece, panels[q], lc, s["land"]["one"][n], s["land"]["two"][n],
                         s["land"]["path"][n], sums[q], s["sum"])
            next(g)
            live.append(g)
            mix.setdefault(q, []).append(g)

    def weight_grad(q, left, right):
        def body(m, _):
            f = 2 * nz * shard
            ms = pl.ds(pl.multiple_of(m * f, f), f)
            v = mm(left(ms), right(), TN)
            panels[q][m // 2, m % 2] = v.astype(BF).reshape(2, nz, shard, width)
            return 0
        lax.fori_loop(0, width // (2 * nz * shard), body, 0)
        start_sums(q)

    py.wait()
    weight_grad(3, lambda ms: SX[0, :, ms], lambda: WD[0][:, :, :low].reshape(rows, width))
    advance((1, 0), (1, 1))
    weight_grad(1, lambda ms: SX[1, :, ms], lambda: LX[1])
    pbx = Load(42, (SV16.at[1], SX.at[0])).start()
    advance((1, 1), (1, 2))
    pump(1, mix[3])
    for m in range(2):
        cp.arrived(NX.at[m], s_h.at[1, m], r_h.at[1, m], p.at(), inner_r)
    pu.wait()
    pb.wait()
    pbx.wait()

    def back_conv(q, _):
        m, c = q // nl, q % nl
        ls = pl.ds(pl.multiple_of(c * lanes, lanes), lanes)
        rs = pl.ds(pl.multiple_of(m * count, count), count)
        v = SX[0, rs, ls].astype(F32)
        prev = PV[m, :, ls].astype(F32)
        dcv = WD[1][m, :, :low, ls].reshape(count, lanes).astype(F32)
        after = NX[m, :, ls].astype(F32)
        mk = masks[m]
        w0, w1, w2 = (dcv * mk[:count, t:t + 1] for t in range(3))
        SG[2:3, ls] += jnp.sum(w0 * earlier(v, prev, 2), axis=0, keepdims=True)
        SG[3:4, ls] += jnp.sum(w1 * earlier(v, prev, 1), axis=0, keepdims=True)
        SG[4:5, ls] += jnp.sum(w2 * v, axis=0, keepdims=True)
        tail = mk[count:count + 8]
        d = GN[2:3, ls] * later(w0, after[:8] * tail[:, 0:1], 2)
        d = d + GN[3:4, ls] * later(w1, after[:8] * tail[:, 1:2], 1)
        d = d + GN[4:5, ls] * w2
        LX[0, rs, ls] = (d * dHa[1, rs, ls]).astype(BF)
        LX[2, rs, ls] = (d * dHa[2, rs, ls]).astype(BF)
        return 0
    lax.fori_loop(0, 2 * nl, back_conv, 0)
    advance((1, 1), (1, 2), (1, 2))
    pump(1, mix[1])
    weight_grad(0, lambda ms: SX[1, :, ms], lambda: LX[0])
    advance((1, 2))
    weight_grad(2, lambda ms: SX[1, :, ms], lambda: LX[2])
    pump(1, mix[0])
    pump(1, mix[3])
    px = Load(42, (x_in, SX.at[1])).start()
    for e, buf, w in ((0, dGb, wbk), (1, dAb, wck)):
        w.wait()
        v = mm(LX[e, :, :half], half_panel(buf, 0), NT) + mm(LX[e, :, half:], half_panel(buf, 1), NT)
        if e == 0:
            dHa[1] = v
            wuk = panel(2, dGb, 23).start()
            pump(1, mix[2])
            pump(1, mix[1])
        else:
            dHa[1] += v
            pump(1, mix[3])
            pump(1, mix[0])
    wuk.wait()
    dHa[1] += mm(LX[2, :, :half], half_panel(dGb, 0), NT) + mm(LX[2, :, half:], half_panel(dGb, 1), NT)
    px.wait()

    def back_one(m, _):
        rs = pl.ds(pl.multiple_of(m * 128, 128), 128)
        inv, n1 = norm(SX[1, rs].astype(F32))
        d = dHa[1, rs]
        SG[0:1] += jnp.sum(d * n1, axis=0, keepdims=True)
        dn = d * GN[0:1]
        SX[0, rs] = (dHa[0, rs] + inv * (dn - n1 * jnp.mean(dn * n1, axis=-1, keepdims=True))).astype(BF)
        return 0
    lax.fori_loop(0, rows // 128, back_one, 0)
    save_gx = Load(30, (SX.at[0], gx_o)).start()
    rest = jnp.zeros((LANES - 8, width), F32)
    GS[...] = jnp.concatenate([SG[...], rest], axis=0).T.astype(BF).reshape(GS.shape)
    start_sums(4)
    pump(1)
    x_add(1, dHa.at[3], 2)

    def finish(m, _):
        rs = pl.ds(pl.multiple_of(m * 128, 128), 128)
        SX[1, rs] = dHa[3, rs].astype(BF)
        return 0
    lax.fori_loop(0, rows // 128, finish, 0)
    save_out = Load(31, (SX.at[1], out_o)).start()
    while live:
        pump(1)
    save_gx.wait()
    save_out.wait()
    for c in own_out:
        c.wait()
    cp.drain()
    ct.drain()
    cx.drain()


def block_call(x, df, masks, blocks, gus, ds, parts, nz, cid):
    rows, width = x.shape
    shard, cols = gus.shape[2], gus.shape[3]
    K = len(parts)
    dr = ds.shape[0]
    V = pl.BlockSpec(memory_space=pltpu.VMEM)
    A = pl.BlockSpec(memory_space=pl.ANY)
    D = pltpu.SemaphoreType.DMA
    M = pltpu.VMEM
    maxc = max(parts) * 2 * nz
    sp = sum_pieces(width)
    ngather = len(gather_pieces(width))
    scratch = dict(
        H=M((2, 2, 2, 2, nz, shard, width), BF),
        dF=M((2, 2, 2, 2, nz, shard, width), BF),
        WGU=M((2, TP, nz, 2, shard, cols), BF),
        WD=[M((2, nz, r, width), BF) for r in parts],
        dHa=M((TP, rows, width), F32),
        Zb=M((TP, 2, 2, nz, shard, cols), BF),
        dAb=M((2, 2, 2, 2, nz, shard, maxc), BF),
        dGb=M((2, 2, 2, 2, nz, shard, maxc), BF),
        GD=[M((2, nz, r, width), BF) for r in parts],
        RY=M((TP, nz, 2, shard, cols), BF),
        ZGU=M((nz, TP, 2, shard, cols), BF),
        ZD=[M((nz, r, width), BF) for r in parts],
        YD=[M((nz, r, width), BF) for r in parts],
        LX=M((4, rows, width), BF),
        SX=M((3, rows, width), BF),
        GN=M((8, width), F32),
        SG=M((8, width), F32),
        SM=M((2, 2, 2, nz, shard, LANES), BF),
        PV=M((2, 16, width), BF),
        NX=M((2, 16, width), BF),
        land=sum_scratch(nz, shard, sp),
        gather=gather_sems(nz, ngather),
        sum=sum_sems(nz, len(sp)),
        sem=D((48,)), sem_h=D((2, 2, 3)), s_h=D((2, 2)), r_h=D((2, 2)),
        s_p0=D((K, 3)), r_p0=D((K, 3)),
        s_z=D((K, 2 * nz)), r_z=D((K, nz)), s_y=D((K, nz)), r_y=D((K, nz)),
        s_dz=D((K, 2, 2 * nz)), r_dz=D((K, 2, nz)), s_dy=D((K,)), r_dy=D((K,)),
        s_gy=D((K, 2, nz)), r_gy=D((K, 2, nz)), s_gz=D((K, 2, nz)), r_gz=D((K, 2, nz)),
        s_gt=D((K, 2, 3)), r_gt=D((K, 2, 3)),
        s_ez=D((K, nz)), r_ez=D((K, nz)), s_ey=D((K, nz)), r_ey=D((K, nz)),
        s_x=D((2, 3)), r_x=D((2, 3)), ready=pltpu.SemaphoreType.REGULAR,
    )
    S = jax.ShapeDtypeStruct
    wide = [width] * 4 + [LANES]
    outs = pl.pallas_call(
        functools.partial(block_body, parts, nz),
        name="block",
        out_shape=[
            S((rows, width), BF), S((rows, width), BF),
            S((TP, 2, shard, cols), BF), S((dr, width), F32),
            *[S((shard, w), F32) for w in (3 * width, width, LANES)],
            *[S((2, 2, 2, nz, shard, w), BF) for w in wide],
            S((5, rows, width), F32), S((3, rows, width), BF),
        ],
        in_specs=[A, A] + [V] * 6 + [A, A],
        out_specs=[A, A, A] + [V] * 4 + [A] * 7,
        scratch_shapes=[scratch],
        compiler_params=pltpu.CompilerParams(
            collective_id=cid, has_side_effects=True, vmem_limit_bytes=67_000_000),
    )(x, df.reshape(2, 2, nz, shard, width), masks, *blocks, gus, ds)
    return outs[:7]


def shifted(block, axis, distance):
    devices = range(lax.axis_size(axis))
    route = [(i - distance, i) for i in devices if i - distance in devices]
    return lax.ppermute(block, axis, route)


def matmul(left, right):
    return jnp.dot(left, right, preferred_element_type=jnp.float32)


def norm_parts(values):
    inverse = lax.rsqrt(jnp.mean(values * values, axis=-1, keepdims=True) + eps)
    return (inverse, values * inverse)


def norm_back(grad_hidden, normed, inverse, gain):
    grad_normed = grad_hidden * gain
    inner_mean = jnp.mean(grad_normed * normed, axis=-1, keepdims=True)
    return inverse * (grad_normed - normed * inner_mean)


def plain_device(
    tokens,
    segments,
    ln1_gain,
    in_weight,
    conv_kernel,
    out_weight,
    ln2_gain,
    gate_weight,
    up_weight,
    down_weight,
    cotangent,
):
    micro_count = tokens.shape[0]
    row_count = tokens.shape[2]
    width = tokens.shape[3]
    taps = conv_kernel.shape[0]
    offset = lax.axis_index("seq") * row_count
    low_gain1 = ln1_gain.astype(jnp.bfloat16)
    low_in = in_weight.astype(jnp.bfloat16)
    low_kernel = conv_kernel.astype(jnp.bfloat16)
    low_out = out_weight.astype(jnp.bfloat16)
    low_gain2 = ln2_gain.astype(jnp.bfloat16)
    low_gate = gate_weight.astype(jnp.bfloat16)
    low_up = up_weight.astype(jnp.bfloat16)
    low_down = down_weight.astype(jnp.bfloat16)
    shard_totals = None
    full_totals = None
    out_list = []
    grad_list = []
    for micro_index in range(micro_count):
        weights = (
            lax.all_gather(low_gain1, ("dp", "seq"), axis=0, tiled=True),
            lax.all_gather(low_in, ("dp", "seq"), axis=0, tiled=True),
            lax.all_gather(low_kernel, ("dp", "seq"), axis=1, tiled=True),
            lax.all_gather(low_out, ("dp", "seq"), axis=0, tiled=True),
            lax.all_gather(low_gain2, ("dp", "seq"), axis=0, tiled=True),
            lax.all_gather(low_gate, ("dp", "seq"), axis=0, tiled=True),
            lax.all_gather(low_up, ("dp", "seq"), axis=0, tiled=True),
            lax.all_gather(low_down, ("dp", "seq"), axis=0, tiled=True),
        )
        gain_one = weights[0].astype(jnp.float32)
        kernel = weights[2].astype(jnp.float32)
        gain_two = weights[4].astype(jnp.float32)
        seg_line = segments[micro_index, 0]
        fill = jnp.full((2,), -1, jnp.int32)
        seg_pad = jnp.concatenate([fill, seg_line, fill])
        window = lax.dynamic_slice_in_dim(seg_pad, offset, row_count + 4)
        masks = [
            (window[tap : tap + row_count + 2] == window[2 : row_count + 4]).astype(jnp.float32)
            for tap in range(taps)
        ]
        tokens_f = tokens[micro_index, 0].astype(jnp.float32)
        inverse_one, normed_one = norm_parts(tokens_f)
        hidden_one = (normed_one * gain_one).astype(jnp.bfloat16)
        projected = matmul(hidden_one, weights[1])
        b_part = projected[:, :width]
        c_part = projected[:, width : 2 * width]
        x_part = projected[:, 2 * width :]
        mixed = (b_part * x_part).astype(jnp.bfloat16)
        prev_rows = shifted(mixed[row_count - 2 :], "seq", 1)
        extended = jnp.concatenate([prev_rows, mixed], axis=0).astype(jnp.float32)
        conv_out = jnp.zeros((row_count, width), jnp.float32)
        for tap in range(taps):
            conv_out = (
                conv_out
                + kernel[tap] * extended[tap : tap + row_count] * masks[tap][:row_count, None]
            )
        gated = (c_part * conv_out).astype(jnp.bfloat16)
        resid = tokens_f + matmul(gated, weights[3])
        inverse_two, normed_two = norm_parts(resid)
        hidden_two = (normed_two * gain_two).astype(jnp.bfloat16)
        gate_pre = matmul(hidden_two, weights[5])
        up_pre = matmul(hidden_two, weights[6])
        sigmoid_gate = jax.nn.sigmoid(gate_pre)
        activated = gate_pre * sigmoid_gate
        inner = (activated * up_pre).astype(jnp.bfloat16)
        ffn_out = matmul(inner, weights[7])
        out_list.append((resid + ffn_out).astype(jnp.bfloat16))
        back_weights = (
            lax.all_gather(low_gain1, ("dp", "seq"), axis=0, tiled=True),
            lax.all_gather(low_in, ("dp", "seq"), axis=0, tiled=True),
            lax.all_gather(low_kernel, ("dp", "seq"), axis=1, tiled=True),
            lax.all_gather(low_out, ("dp", "seq"), axis=0, tiled=True),
            lax.all_gather(low_gain2, ("dp", "seq"), axis=0, tiled=True),
            lax.all_gather(low_gate, ("dp", "seq"), axis=0, tiled=True),
            lax.all_gather(low_up, ("dp", "seq"), axis=0, tiled=True),
            lax.all_gather(low_down, ("dp", "seq"), axis=0, tiled=True),
        )
        grad_final = cotangent[micro_index, 0]
        grad_inner = matmul(grad_final, back_weights[7].T)
        part_down = matmul(inner.T, grad_final)
        grad_gate_pre = (
            grad_inner * up_pre * sigmoid_gate * (1.0 + gate_pre * (1.0 - sigmoid_gate))
        ).astype(jnp.bfloat16)
        grad_up_pre = (grad_inner * activated).astype(jnp.bfloat16)
        grad_hidden_two = matmul(grad_gate_pre, back_weights[5].T) + matmul(
            grad_up_pre, back_weights[6].T
        )
        part_gate = matmul(hidden_two.T, grad_gate_pre)
        part_up = matmul(hidden_two.T, grad_up_pre)
        part_gain2 = jnp.sum(grad_hidden_two * normed_two, axis=0)
        grad_resid = grad_final.astype(jnp.float32) + norm_back(
            grad_hidden_two, normed_two, inverse_two, gain_two
        )
        grad_branch = grad_resid.astype(jnp.bfloat16)
        grad_gated = matmul(grad_branch, back_weights[3].T)
        part_out = matmul(gated.T, grad_branch)
        grad_c = grad_gated * conv_out
        grad_conv = (grad_gated * c_part).astype(jnp.bfloat16)
        next_rows = shifted(grad_conv[:2], "seq", -1)
        grad_extended = jnp.concatenate([grad_conv, next_rows], axis=0).astype(jnp.float32)
        grad_mixed = jnp.zeros((row_count, width), jnp.float32)
        kernel_terms = []
        for tap in range(taps):
            weighted = grad_extended * masks[tap][:, None]
            grad_mixed = grad_mixed + kernel[tap] * weighted[2 - tap : 2 - tap + row_count]
            kernel_terms.append(
                jnp.sum(weighted[:row_count] * extended[tap : tap + row_count], axis=0)
            )
        part_kernel = jnp.stack(kernel_terms, axis=0)
        grad_proj = jnp.concatenate(
            [grad_mixed * x_part, grad_c, grad_mixed * b_part], axis=1
        ).astype(jnp.bfloat16)
        grad_hidden_one = matmul(grad_proj, back_weights[1].T)
        part_in = matmul(hidden_one.T, grad_proj)
        part_gain1 = jnp.sum(grad_hidden_one * normed_one, axis=0)
        grad_input = grad_resid + norm_back(grad_hidden_one, normed_one, inverse_one, gain_one)
        grad_list.append(grad_input.astype(jnp.bfloat16))
        parts = (
            part_gain1,
            part_in,
            part_kernel,
            part_out,
            part_gain2,
            part_gate,
            part_up,
            part_down,
        )
        full_totals = (
            parts
            if full_totals is None
            else tuple((first + second for first, second in zip(full_totals, parts)))
        )
    shard_totals = (
        lax.psum_scatter(full_totals[0], ("dp", "seq"), scatter_dimension=0, tiled=True),
        lax.psum_scatter(full_totals[1], ("dp", "seq"), scatter_dimension=0, tiled=True),
        lax.psum_scatter(full_totals[2], ("dp", "seq"), scatter_dimension=1, tiled=True),
        lax.psum_scatter(full_totals[3], ("dp", "seq"), scatter_dimension=0, tiled=True),
        lax.psum_scatter(full_totals[4], ("dp", "seq"), scatter_dimension=0, tiled=True),
        lax.psum_scatter(full_totals[5], ("dp", "seq"), scatter_dimension=0, tiled=True),
        lax.psum_scatter(full_totals[6], ("dp", "seq"), scatter_dimension=0, tiled=True),
        lax.psum_scatter(full_totals[7], ("dp", "seq"), scatter_dimension=0, tiled=True),
    )
    output = jnp.stack(out_list, axis=0)[:, None]
    grad_tokens = jnp.stack(grad_list, axis=0)[:, None]
    return (
        output,
        grad_tokens,
        shard_totals[0],
        shard_totals[1],
        shard_totals[2],
        shard_totals[3],
        shard_totals[4],
        shard_totals[5],
        shard_totals[6],
        shard_totals[7],
    )


def cut_columns(w, parts, ny, nz):
    rows, shard = w.shape[0], w.shape[1] // (ny * TP * nz)
    cut = w.astype(BF).reshape(rows, ny, TP, nz, shard)
    pieces, start = [], 0
    for size in parts:
        piece = cut[..., start : start + size].transpose(2, 0, 1, 3, 4)
        pieces.append(piece.reshape(TP, rows, ny * nz * size))
        start += size
    return jnp.concatenate(pieces, axis=-1)


def join_columns(g, parts, ny, nz):
    rows = g.shape[1]
    pieces, start, npos = [], 0, ny * nz
    for size in parts:
        piece = g[:, :, npos * start : npos * (start + size)].reshape(TP, rows, ny, nz, size)
        pieces.append(piece.transpose(1, 2, 0, 3, 4))
        start += size
    return jnp.concatenate(pieces, axis=-1).reshape(rows, -1).astype(F32)


def fast_device(
    parts,
    tokens,
    segments,
    ln1_gain,
    in_weight,
    conv_kernel,
    out_weight,
    ln2_gain,
    gate_weight,
    up_weight,
    down_weight,
    cotangent,
):
    micro, _, count, width = tokens.shape
    taps = conv_kernel.shape[0]
    nz = lax.axis_size("seq")
    ny = lax.axis_size("dp") // TP
    rows = micro * count
    low_in = in_weight.astype(BF)
    small = jnp.concatenate([ln1_gain[None], ln2_gain[None], conv_kernel], axis=0).astype(BF)
    small = jnp.pad(small.T, ((0, 0), (0, LANES - taps - 2)))
    blocks = [low_in[:, q * width : (q + 1) * width] for q in range(3)]
    blocks += [out_weight.astype(BF), small]
    offset = lax.axis_index("seq") * count
    fill = jnp.full((micro, 2), -1, jnp.int32)
    seg_pad = jnp.concatenate([fill, segments[:, 0], fill, fill, fill, fill], axis=1)
    window = lax.dynamic_slice_in_dim(seg_pad, offset, count + 10, axis=1)
    masks = jnp.stack(
        [window[:, tap : tap + count + 8] == window[:, 2 : count + 10] for tap in range(taps)], axis=-1
    ).astype(F32)
    masks = jnp.pad(masks, ((0, 0), (0, 0), (0, LANES - taps)))
    gus = jnp.stack([cut_columns(w, parts, ny, nz) for w in (gate_weight, up_weight)], axis=1)
    output, gx, gu, gd, g_in, g_out, g_small = block_call(
        tokens.reshape(rows, width), cotangent.reshape(rows, width), masks, blocks, gus,
        down_weight.astype(BF), parts, nz, 0
    )
    g_gate = join_columns(gu[:, 0], parts, ny, nz)
    g_up = join_columns(gu[:, 1], parts, ny, nz)
    g_small = g_small[:, : taps + 2].T
    shape = tokens.shape
    return (
        output.reshape(shape), gx.reshape(shape), g_small[0], g_in, g_small[2:], g_out,
        g_small[1], g_gate, g_up, gd,
    )


def row_parts(mesh, token_shape, down_shape):
    nd, nz = mesh.shape["dp"], mesh.shape["seq"]
    if nd != 2 * TP:
        return None
    per = down_shape[0] // (nd * nz)
    shard = token_shape[3] // (nd * nz)
    rows = token_shape[0] * (token_shape[2] // nz)
    if per <= 64 or per % 16 or shard % 16 or token_shape[1] != nd or token_shape[0] != 2:
        return None
    if rows != 4 * nz * shard or token_shape[3] != 2 * rows or 128 * nz != rows:
        return None
    return (per - 64, 64)


def solution(mesh):
    in_specs = (
        P(None, "dp", "seq", None),
        P(None, "dp", None),
        P(("dp", "seq")),
        P(("dp", "seq"), None),
        P(None, ("dp", "seq")),
        P(("dp", "seq"), None),
        P(("dp", "seq")),
        P(("dp", "seq"), None),
        P(("dp", "seq"), None),
        P(("dp", "seq"), None),
        P(None, "dp", "seq", None),
    )
    out_specs = (
        P(None, "dp", "seq", None),
        P(None, "dp", "seq", None),
        P(("dp", "seq")),
        P(("dp", "seq"), None),
        P(None, ("dp", "seq")),
        P(("dp", "seq"), None),
        P(("dp", "seq")),
        P(("dp", "seq"), None),
        P(("dp", "seq"), None),
        P(("dp", "seq"), None),
    )

    def run(*arrays):
        parts = row_parts(mesh, arrays[0].shape, arrays[9].shape)
        device = plain_device if parts is None else functools.partial(fast_device, parts)
        return jax.shard_map(
            device, mesh=mesh, in_specs=in_specs, out_specs=out_specs, check_vma=False
        )(*arrays)

    return run
```

profile of v0, /device:TPU:0, one launch (start us, length us, event | category | flops | bytes accessed | tf_op | source)
XLA Modules:
  0.0 326.5 jit_solution(577203066882967079)
XLA Ops:
  0.7 0.1 pad.28.clone
  0.7 0.7 convert.17
  1.5 0.7 convert_bitcast_fusion
  2.2 0.1 copy.102
  2.3 0.6 pad.12.b4
  2.9 0.7 copy.134
  3.6 0.1 concatenate.19
  3.7 0.1 compare_bitcast_fusion.1
  3.8 1.5 convert_element_type.34.b3
  5.3 0.2 copy.100
  5.5 0.2 copy.101
  5.7 0.1 add_add_fusion
  5.9 1.0 convert_element_type.33
  6.9 0.7 fusion
  7.6 0.7 pad_convert_fusion.masks
  8.4 0.9 reshape.66
  9.3 0.1 copy_bitcast_fusion.3
  9.4 0.2 copy_bitcast_fusion.2
  9.6 0.2 reshape.68
  9.8 0.2 reshape.67
  10.0 0.9 reshape.69
  10.9 0.1 copy_bitcast_fusion.1
  11.0 0.2 copy_bitcast_fusion
  11.2 0.2 reshape.71
  11.5 0.2 reshape.70
  11.7 0.9 pad_maximum_fusion.gus
  12.6 0.8 convert_element_type.37.ds
  13.4 298.9 %block.1 = (bf16[512,1024]{1,0:T(8,128)(2,1)}, bf16[512,1024]{1,0:T(8,128)(2,1)}, bf16[4,2,32,1152]{3,2,1,0:T(8,128)(2,1)}, f32[144,1024]{1,0:T(8,128)}, f32[32,...) custom-call(bf16[512,1024]{1,0:T(8,128)(2,1)} %bitcast.51, ...), custom_call_target="tpu_custom_call" | custom-call | tf_op jit(solution)/shard_map/block/pallas_call | solution.py:1011
  312.2 0.7 slice_bitcast_fusion.2
  313.0 0.7 slice_reduce_fusion
  313.7 0.1 slice.91
  313.7 0.7 copy.115
  314.4 1.1 slice_bitcast_fusion
  315.5 0.3 reshape.76
  315.9 0.2 reshape.77
  316.1 0.3 reshape.74
  316.5 0.2 reshape.75
  316.7 0.2 maximum_convert_fusion
  316.9 0.7 copy.109
  317.6 1.8 reshape.78
  319.4 0.2 maximum_convert_fusion.1
  319.6 0.7 copy.112
  320.3 1.8 reshape.79
  322.1 1.0 copy.140
  323.1 1.0 copy.141
  324.0 0.7 copy.142
  324.8 0.7 copy.143
  325.4 0.8 copy.144
  (30 shorter events, 0.4 us)
Async XLA Ops:
  0.6 7.7 %copy-start.2 = (f32[32,4608]{1,0:T(8,128)S(1)}, f32[32,4608]{1,0:T(8,128)}, u32[]{:S(2)}) copy-start(f32[32,4608]{1,0:T(8,128)} %param.18) | copy-start | bytes 1769476
  6.9 3.1 copy-start.3
  10.9 1.7 copy-start.4
  319.6 2.5 copy-start.1
  320.3 2.7 copy-start
  322.1 2.0 copy-start.6
  322.1 2.7 copy-start.7
  323.1 2.4 copy-start.5
where the time goes:
time: 331 us; the launch traced here: 326 us
  Pallas kernels  299 us (90%)
  local copies, waits for them, and re-layouts  19.3 us (6%)
  other arithmetic  7.17 us (2%)
    pallas_call x1, Pallas kernels, block_call(): pl.pallas_call(functools.partial(block_body, parts, nz), name='block', ou...  299 us

commit v1 on v0

--- a/solution.py
+++ b/solution.py
@@ -99,7 +99,7 @@
     there = [p.at(i=p.member(t)) for t in range(1, TP)] + [p.at(y=1 - p.y)] + [p.at(z=q) for q in p.others]
     for device in there:
         pl.semaphore_signal(bar, inc=1, device_id=device, device_id_type=MESH)
-    pl.semaphore_wait(bar, len(there))
+    return lambda: pl.semaphore_wait(bar, len(there))
 
 
 def gather_pieces(width):
@@ -242,15 +242,17 @@
     LZ[z] = jnp.zeros(LZ.shape[1:], BF)
     yield
     cp.arrived(LC, s_c.at[n], r_c.at[n], p.at())
+    def add_core(bb):
+        def one(zz, _):
+            for aa in range(2):
+                i = g(bb, aa, zz)
+                G[i] = (f(G[i]) + f(LC[lc(bb, aa, zz)])).astype(BF)
+            return 0
+        lax.fori_loop(0, p.nz, one, 0)
+    add_core(1 - b)
     for zz in targets:
-        for aa in range(2):
-            i = g(1 - b, aa, zz)
-            G[i] = (f(G[i]) + f(LC[lc(1 - b, aa, zz)])).astype(BF)
         cp.send(row(1 - b, zz), L1.at[:, zz], s_1.at[n, zz], r_1.at[n, zz], dev_b)
-    for zz in targets:
-        for aa in range(2):
-            i = g(b, aa, zz)
-            G[i] = (f(G[i]) + f(LC[lc(b, aa, zz)])).astype(BF)
+    add_core(b)
     if zlast:
         yield
         for zz in targets:
@@ -347,13 +349,13 @@
             for c in self.copies:
                 c.wait()
 
+    all_here = entry_barrier(p)
     own_w = Load(0, *[(b, w.at[p.y, p.x, p.c, z]) for b, w in zip((b0, b1, b2, b3, b4), W)]).start()
     own_x = Load(5, (x_in, SX.at[0])).start()
     df_blocks = df_in
     own_df = Load(6, (df_blocks, slot(dF, 0))).start()
     own_gu = Load(7, (gus.at[p.i], WGU.at[p.y, p.i, z])).start()
     own_d = Load(8, *[(ds.at[rws(k)], WD[k].at[p.y, z]) for k in range(K)]).start()
-    entry_barrier(p)
 
     ZGU[z] = jnp.zeros(ZGU.shape[1:], BF)
     for k in range(K):
@@ -429,20 +431,26 @@
         for zz in p.others[::-1]:
             yield
             cp.arrived(RY.at[:, zz, w, :, c], s_gy.at[k, w, zz], r_gy.at[k, w, zz], p.at())
-            for j in range(TP):
+
+            def add(j, _, zz=zz):
                 GGU[p.y, j, zz, w, :, c] = (
                     GGU[p.y, j, zz, w, :, c].astype(F32) + RY[j, zz, w, :, c].astype(F32)).astype(BF)
+                return 0
+            lax.fori_loop(0, TP, add, 0)
             cp.send(GGU.at[p.y, :, zz, w, :, c], ZGU.at[z, :, w, :, c], s_gz.at[k, w, zz], r_gz.at[k, w, z],
                     p.at(z=zz))
         yield
         cp.arrived(RY.at[:, z, w, :, c], s_gy.at[k, w, z], r_gy.at[k, w, z], p.at())
         for zz in p.others:
             cp.arrived(ZGU.at[zz, :, w, :, c], s_gz.at[k, w, zz], r_gz.at[k, w, zz], p.at())
-        for j in range(TP):
+
+        def add_all(j, _):
             v = GGU[p.y, j, z, w, :, c].astype(F32) + RY[j, z, w, :, c].astype(F32)
             for zz in range(nz):
                 v = v + ZGU[zz, j, w, :, c].astype(F32)
             GGU[p.y, j, z, w, :, c] = v.astype(BF)
+            return 0
+        lax.fori_loop(0, TP, add_all, 0)
         for t in (2, 3, 1):
             m = p.member(t)
             cp.send(GGU.at[p.y, m, z, w, :, c], ogu_o.at[p.i, w, :, c], s_gt.at[k, w, t - 1], r_gt.at[k, w, t - 1],
@@ -487,6 +495,7 @@
                 live.remove(g)
 
     own_w.wait()
+    all_here()
     gp = gather_pieces(width)
     gather = [gather_flow(p, cp, n, q, W[q[0]], s["gather"]) for n, q in enumerate(gp)]
     states = {}
@@ -666,15 +675,23 @@
             return 0
         lax.fori_loop(0, 2, some, 0)
 
-    def ffn_out(t, put):
-        def some(r, _):
+    def slots(k, start, step):
+        def one(n, _):
+            fwd_mid(k, start + step * n)
+            return 0
+        lax.fori_loop(0, 2, one, 0)
+
+    def ffn_out(slot_of, put):
+        def some(q, _):
+            n, r = q // 2, q % 2
+            t = slot_of(n)
             f = None
             for k in range(K):
                 v = mm(Zb[t, r, :, :, :, cols(k)].reshape(count, CH[k][1]), WD[k][...].reshape(CH[k][1], width), NN)
                 f = v if f is None else f + v
-            put(pl.ds(pl.multiple_of(r * count, count), count), f)
+            put(n, pl.ds(pl.multiple_of(r * count, count), count), f)
             return 0
-        lax.fori_loop(0, 2, some, 0)
+        lax.fori_loop(0, 4, some, 0)
 
     tok = TP * rows
 
@@ -746,25 +763,23 @@
         if k == 0:
             acts_wait(H, 0, 1)
             acts_wait(dF, 1, 1)
-            fwd_mid(0, 0)
-            fwd_mid(0, 1)
+            slots(0, 0, 1)
             acts_forward(H, 0)
             acts_wait(dF, 1, 3)
-            fwd_mid(0, 2)
             acts_wait(H, 0, 3)
-            fwd_mid(0, 3)
+            slots(0, 2, 1)
             pump(1, ag[1:2])
         else:
-            for t in (3, 2, 1, 0):
-                fwd_mid(k, t)
-                if k == K - 1 and t == 3:
-                    x_send1(0, 1, dHa[3])
-                if k == K - 1 and t == 2:
-                    x_send2(0, dHa.at[2])
-                if k == K - 1 and t == 1:
-                    x_send1(0, 0, dHa[1])
-                if k == 1:
-                    advance(*{3: (), 2: ((0, 0),), 1: ((0, 0),), 0: ((0, 0), (0, 1))}[t])
+            slots(k, 3, -1)
+            if k == K - 1:
+                x_send1(0, 1, dHa[3])
+                advance((0, 0))
+                x_send2(0, dHa.at[2])
+                advance((0, 0))
+            slots(k, 1, -1)
+            if k == K - 1:
+                x_send1(0, 0, dHa[1])
+                advance((0, 0), (0, 1))
         cg[k].drain()
         before = len(cp.pending)
         grads(k)
@@ -772,29 +787,20 @@
     x_add(0, dHa.at[0], 0)
     pl.semaphore_signal(s["ready"], inc=1, device_id=p.at(i=p.member(1)), device_id_type=MESH)
     pr = Load(40, (SV32.at[4], dHa.at[2])).start()
-    advance((0, 1), (0, 2), (0, 2))
-
-    def keep(n):
-        def put(rs, v):
-            dHa[n, rs] = v
-        return put
-
-    def stage(e):
-        def put(rs, v):
-            SX[e, rs] = v.astype(BF)
-        return put
-    ffn_out(2, keep(1))
-    ffn_out(0, keep(3))
-    advance((0, 1), (0, 2), (1, 0))
+
+    def keep(n, rs, v):
+        dHa[1 + 2 * n, rs] = v
+
+    def stage(n, rs, v):
+        SX[n, rs] = v.astype(BF)
+    ffn_out(lambda n: 2 - 2 * n, keep)
     cx.drain(1)
     cx.pending.append(cx.pending.pop(0))
     cx.drain(1)
-    ffn_out(1, stage(0))
-    ffn_out(3, stage(1))
+    ffn_out(lambda n: 1 + 2 * n, stage)
     pl.semaphore_wait(s["ready"], 1)
     x_send1(1, 0)
     x_send1(1, 1)
-    advance((1, 0))
     x_add(0, dHa.at[0], 2)
     cx.drain(1)
     x_send2(1, dHa.at[1])
@@ -822,7 +828,7 @@
         return 0
     lax.fori_loop(0, 4, back_two, 0)
     pcv = Load(44, (SV32.at[3], dHa.at[2])).start()
-    advance((1, 0), (1, 1))
+    advance((1, 0))
     wo.wait()
     pc.wait()
     pcv.wait()
@@ -836,7 +842,7 @@
         WD[1][m, :, :low] = (dy * dHa[1, rs]).astype(BF).reshape(nz, low, width)
         return 0
     lax.fori_loop(0, 2, back_y, 0)
-    advance((1, 0), (1, 1))
+    advance((1, 0))
     wck = panel(1, dAb, 21).start()
     for m in range(2):
         cp.send(WD[1].at[m, 0, pl.ds(0, 16)], NX.at[m], s_h.at[1, m], r_h.at[1, m], p.at(z=z - 1), inner_l)
@@ -875,7 +881,7 @@
     advance((1, 0), (1, 1))
     weight_grad(1, lambda ms: SX[1, :, ms], lambda: LX[1])
     pbx = Load(42, (SV16.at[1], SX.at[0])).start()
-    advance((1, 1), (1, 2))
+    advance((1, 1))
     pump(1, mix[3])
     for m in range(2):
         cp.arrived(NX.at[m], s_h.at[1, m], r_h.at[1, m], p.at(), inner_r)
@@ -907,7 +913,7 @@
     advance((1, 1), (1, 2), (1, 2))
     pump(1, mix[1])
     weight_grad(0, lambda ms: SX[1, :, ms], lambda: LX[0])
-    advance((1, 2))
+    advance((1, 2), (0, 2), (0, 2))
     weight_grad(2, lambda ms: SX[1, :, ms], lambda: LX[2])
     pump(1, mix[0])
     pump(1, mix[3])

time: 331 us -> 308 us (0.931)
  Pallas kernels: 299 us -> 274 us
    pallas_call x1, Pallas kernels: 299 us -> 274 us  [block_call(): pl.pallas_call(functools.partial(block_body, parts, nz), name='block', ou...]
where the time goes in v1:
time: 308 us; the launch traced here: 302 us
  Pallas kernels  274 us (89%)
  local copies, waits for them, and re-layouts  19.3 us (6%)
  other arithmetic  7.17 us (2%)
    pallas_call x1, Pallas kernels, block_call(): pl.pallas_call(functools.partial(block_body, parts, nz), name='block', ou...  274 us

profile of v1, /device:TPU:0, one launch (start us, length us, event | category | flops | bytes accessed | tf_op | source)
XLA Modules:
  0.0 301.8 jit_solution(9206204298828439563)
XLA Ops:
  0.7 0.1 pad.28.clone
  0.7 0.7 convert.17
  1.5 0.7 convert_bitcast_fusion
  2.2 0.1 copy.102
  2.3 0.6 pad.12.b4
  2.9 0.7 copy.134
  3.6 0.1 concatenate.19
  3.7 0.1 compare_bitcast_fusion.1
  3.8 1.5 convert_element_type.34.b3
  5.3 0.2 copy.100
  5.5 0.2 copy.101
  5.7 0.1 add_add_fusion
  5.9 1.0 convert_element_type.33
  6.9 0.7 fusion
  7.6 0.7 pad_convert_fusion.masks
  8.4 0.9 reshape.66
  9.3 0.1 copy_bitcast_fusion.3
  9.4 0.2 copy_bitcast_fusion.2
  9.6 0.2 reshape.68
  9.8 0.2 reshape.67
  10.0 0.9 reshape.69
  10.9 0.1 copy_bitcast_fusion.1
  11.0 0.2 copy_bitcast_fusion
  11.2 0.2 reshape.71
  11.5 0.2 reshape.70
  11.7 0.9 pad_maximum_fusion.gus
  12.6 0.8 convert_element_type.37.ds
  13.4 274.2 %block.1 = (bf16[512,1024]{1,0:T(8,128)(2,1)}, bf16[512,1024]{1,0:T(8,128)(2,1)}, bf16[4,2,32,1152]{3,2,1,0:T(8,128)(2,1)}, f32[144,1024]{1,0:T(8,128)}, f32[32,...) custom-call(bf16[512,1024]{1,0:T(8,128)(2,1)} %bitcast.51, ...), custom_call_target="tpu_custom_call" | custom-call | tf_op jit(solution)/shard_map/block/pallas_call | solution.py:1017
  287.6 0.7 slice_bitcast_fusion.2
  288.3 0.7 slice_reduce_fusion
  289.0 0.1 slice.91
  289.1 0.7 copy.115
  289.7 1.1 slice_bitcast_fusion
  290.9 0.3 reshape.76
  291.2 0.2 reshape.77
  291.5 0.3 reshape.74
  291.8 0.2 reshape.75
  292.0 0.2 maximum_convert_fusion
  292.3 0.7 copy.109
  293.0 1.8 reshape.78
  294.7 0.2 maximum_convert_fusion.1
  295.0 0.7 copy.112
  295.7 1.8 reshape.79
  297.4 1.0 copy.140
  298.4 1.0 copy.141
  299.4 0.7 copy.142
  300.1 0.7 copy.143
  300.8 0.8 copy.144
  (30 shorter events, 0.4 us)
Async XLA Ops:
  0.6 7.7 %copy-start.2 = (f32[32,4608]{1,0:T(8,128)S(1)}, f32[32,4608]{1,0:T(8,128)}, u32[]{:S(2)}) copy-start(f32[32,4608]{1,0:T(8,128)} %param.18) | copy-start | bytes 1769476
  6.9 3.1 %copy-start.3 = (f32[32,4608]{1,0:T(8,128)S(1)}, f32[32,4608]{1,0:T(8,128)}, u32[]{:S(2)}) copy-start(f32[32,4608]{1,0:T(8,128)} %param.19) | copy-start | bytes 1769476
  10.9 1.7 copy-start.4
  295.0 2.5 copy-start.1
  295.7 2.7 copy-start
  297.4 2.0 copy-start.6
  297.4 2.7 copy-start.7
  298.4 2.4 copy-start.5

commit v2 on v1

--- a/solution.py
+++ b/solution.py
@@ -31,6 +31,7 @@
 class Place:
     def __init__(self, nz):
         dp = lax.axis_index("dp")
+        self.dp = dp
         self.y = dp // TP
         self.i = dp % TP
         self.z = lax.axis_index("seq")
@@ -60,9 +61,11 @@
         return x * 2 + c
 
     def at(self, y=None, i=None, z=None):
+        z = self.z if z is None else z
+        if y is None and i is None:
+            return (self.dp, z)
         y = self.y if y is None else y
         i = self.i if i is None else i
-        z = self.z if z is None else z
         return (y * TP + i, z)
 
 
@@ -103,13 +106,12 @@
 
 
 def gather_pieces(width):
-    half = width // 2
     return (
         (4, 0, LANES, "zyx"),
-        (0, 0, half, "zyx"), (0, half, half, "zxy"),
-        (2, 0, half, "xzy"), (2, half, half, "yzx"),
-        (1, 0, half, "zyx"), (1, half, half, "zxy"),
-        (3, 0, half, "xzy"), (3, half, half, "yzx"),
+        (0, 0, width, "zyx"),
+        (2, 0, width, "xzy"),
+        (1, 0, width, "zxy"),
+        (3, 0, width, "yzx"),
     )
 
 
@@ -315,6 +317,7 @@
     K = len(parts)
     cp, cx, ct = Copies(), Copies(), Copies()
     cg = [Copies() for _ in range(K)]
+    core_dev, x_dev = p.at(i=p.member(1)), p.at(i=p.member(2))
     first, last = z == 0, z == nz - 1
     inner_l, inner_r = z > 0, z < nz - 1
     H, dF, WGU, WD, dHa, Zb, dAb, dGb = (s[k] for k in ("H", "dF", "WGU", "WD", "dHa", "Zb", "dAb", "dGb"))
@@ -384,7 +387,12 @@
 
     def acts_forward(dst, q):
         acts_wait(dst, q, 2)
-        cp.send(slot(dst, 2), slot(dst, 3), sem_h.at[q, 0, 2], sem_h.at[q, 1, 2], p.at(i=p.member(1)))
+        cp.send(slot(dst, 2), slot(dst, 3), sem_h.at[q, 0, 2], sem_h.at[q, 1, 2], core_dev, group=True)
+
+    def acts_forwarded(dst, q):
+        cp.pending.append((True, lambda: pltpu.make_async_remote_copy(
+            src_ref=slot(dst, 2), dst_ref=slot(dst, 3), send_sem=sem_h.at[q, 0, 2], recv_sem=sem_h.at[q, 1, 2],
+            device_id=core_dev, device_id_type=MESH)))
 
     def gu_blk(k, y, zz):
         return WGU.at[y, :, zz, :, :, cols(k)]
@@ -558,8 +566,10 @@
     save_h1 = Load(30, (SX.at[1], SV16.at[0])).start()
 
     def project(buf, dst):
-        for h in range(2):
-            dHa[dst, :, h * half:(h + 1) * half] = mm(SX[1], half_panel(buf, h), NN)
+        def one(h, _):
+            dHa[dst, :, pl.ds(pl.multiple_of(h * half, half), half)] = mm(SX[1], half_panel(buf, h), NN)
+            return 0
+        lax.fori_loop(0, 2, one, 0)
     need(2)
     wu = panel(2, dGb, 23).start()
     wb.wait()
@@ -625,9 +635,12 @@
     save_bu.wait()
     pump(1, ag)
     wo.wait()
-    for h in range(2):
-        hs = slice(h * half, (h + 1) * half)
+
+    def residual(h, _):
+        hs = pl.ds(pl.multiple_of(h * half, half), half)
         dHa[0, :, hs] = SX[0, :, hs].astype(F32) + mm(LX[0], half_panel(dGb, h), NN)
+        return 0
+    lax.fori_loop(0, 2, residual, 0)
 
     def norm_two(m, _):
         rs = pl.ds(pl.multiple_of(m * nz * shard, nz * shard), nz * shard)
@@ -675,12 +688,6 @@
             return 0
         lax.fori_loop(0, 2, some, 0)
 
-    def slots(k, start, step):
-        def one(n, _):
-            fwd_mid(k, start + step * n)
-            return 0
-        lax.fori_loop(0, 2, one, 0)
-
     def ffn_out(slot_of, put):
         def some(q, _):
             n, r = q // 2, q % 2
@@ -711,6 +718,16 @@
             if k == K - 1:
                 advance(*(((0, 0), (0, 1)) if w == 0 else ((0, 0), (0, 1), (0, 2))))
         r = parts[k]
+        if 128 % r == 0 and (nz * r) % 128 == 0:
+            def down(b, _):
+                ls = pl.ds(pl.multiple_of(c0 + b * 128, 128), 128)
+                v = mm(Zb[:, :, :, :, :, ls].reshape(tok, 128), dF[...].reshape(tok, width), TN).astype(BF)
+                n, per = 128 // r, nz * r // 128
+                GD[k][b // per, pl.ds((b % per) * n, n)] = v.reshape(n, r, width)
+                return 0
+            lax.fori_loop(0, cn // 128, down, 0)
+            begin((k, 2), flow_rs_d(k))
+            return
         for b in range(cn // 128):
             zb = Zb[:, :, :, :, :, c0 + b * 128:c0 + (b + 1) * 128].reshape(tok, 128)
             v = mm(zb, dF[...].reshape(tok, width), TN).astype(BF)
@@ -740,7 +757,12 @@
     def x_send1(q, e, value=None):
         if value is not None:
             SX[e] = value.astype(BF)
-        cx.send(SX.at[e], x_land(q, e), s_x.at[q, e], r_x.at[q, e], p.at(i=p.member(1)))
+        cx.send(SX.at[e], x_land(q, e), s_x.at[q, e], r_x.at[q, e], core_dev, group=True)
+
+    def x_sent(q, e):
+        cx.pending.append((True, lambda: pltpu.make_async_remote_copy(
+            src_ref=SX.at[e], dst_ref=x_land(q, e), send_sem=s_x.at[q, e], recv_sem=r_x.at[q, e],
+            device_id=x_dev if e == 2 else core_dev, device_id_type=MESH)))
 
     def x_wait(q, e):
         cx.arrived(x_land(q, e), s_x.at[q, e], r_x.at[q, e], p.at(i=p.member(2 if e == 2 else 1)))
@@ -748,13 +770,14 @@
     def x_send2(q, acc):
         x_wait(q, 1)
         SX[2] = (acc[...] + LX[1].astype(F32)).astype(BF)
-        cx.send(SX.at[2], x_land(q, 2), s_x.at[q, 2], r_x.at[q, 2], p.at(i=p.member(2)))
+        cx.send(SX.at[2], x_land(q, 2), s_x.at[q, 2], r_x.at[q, 2], x_dev, group=True)
 
     def x_add(q, acc, e):
         x_wait(q, e)
         acc[...] += x_land(q, e)[...].astype(F32)
 
     acts_forward(dF, 1)
+    acts_forwarded(dF, 1)
     before = 0
     for k in range(K):
         run(ag[k])
@@ -763,23 +786,34 @@
         if k == 0:
             acts_wait(H, 0, 1)
             acts_wait(dF, 1, 1)
-            slots(0, 0, 1)
-            acts_forward(H, 0)
-            acts_wait(dF, 1, 3)
-            acts_wait(H, 0, 3)
-            slots(0, 2, 1)
+            def others_here():
+                acts_forward(H, 0)
+                acts_wait(dF, 1, 3)
+                acts_wait(H, 0, 3)
+
+            def one(t, _):
+                pl.when(t == 2)(others_here)
+                fwd_mid(0, t)
+                return 0
+            lax.fori_loop(0, TP, one, 0)
+            acts_forwarded(H, 0)
             pump(1, ag[1:2])
         else:
-            slots(k, 3, -1)
-            if k == K - 1:
+            def sums_out():
                 x_send1(0, 1, dHa[3])
-                advance((0, 0))
                 x_send2(0, dHa.at[2])
-                advance((0, 0))
-            slots(k, 1, -1)
+
+            def one(n, _, k=k):
+                fwd_mid(k, TP - 1 - n)
+                if k == K - 1:
+                    pl.when(n == 1)(sums_out)
+                return 0
+            lax.fori_loop(0, TP, one, 0)
             if k == K - 1:
                 x_send1(0, 0, dHa[1])
-                advance((0, 0), (0, 1))
+                for e in (1, 2, 0):
+                    x_sent(0, e)
+                advance((0, 0), (0, 0), (0, 0), (0, 1))
         cg[k].drain()
         before = len(cp.pending)
         grads(k)
@@ -801,9 +835,12 @@
     pl.semaphore_wait(s["ready"], 1)
     x_send1(1, 0)
     x_send1(1, 1)
+    x_sent(1, 0)
+    x_sent(1, 1)
     x_add(0, dHa.at[0], 2)
     cx.drain(1)
     x_send2(1, dHa.at[1])
+    x_sent(1, 2)
     x_add(1, dHa.at[3], 0)
 
     pc = Load(41, (SV32.at[1], dHa.at[1])).start()
@@ -918,20 +955,28 @@
     pump(1, mix[0])
     pump(1, mix[3])
     px = Load(42, (x_in, SX.at[1])).start()
-    for e, buf, w in ((0, dGb, wbk), (1, dAb, wck)):
-        w.wait()
-        v = mm(LX[e, :, :half], half_panel(buf, 0), NT) + mm(LX[e, :, half:], half_panel(buf, 1), NT)
-        if e == 0:
-            dHa[1] = v
-            wuk = panel(2, dGb, 23).start()
-            pump(1, mix[2])
-            pump(1, mix[1])
-        else:
-            dHa[1] += v
-            pump(1, mix[3])
-            pump(1, mix[0])
+
+    def back_in(e, buf):
+        def one(m, _):
+            rs = pl.ds(pl.multiple_of(m * count, count), count)
+            v = mm(LX[e, rs, :half], half_panel(buf, 0), NT) + mm(LX[e, rs, half:], half_panel(buf, 1), NT)
+            if e == 0:
+                dHa[1, rs] = v
+            else:
+                dHa[1, rs] += v
+            return 0
+        lax.fori_loop(0, 2, one, 0)
+    wbk.wait()
+    back_in(0, dGb)
+    wuk = panel(2, dGb, 23).start()
+    pump(1, mix[2])
+    pump(1, mix[1])
+    wck.wait()
+    back_in(1, dAb)
+    pump(1, mix[3])
+    pump(1, mix[0])
     wuk.wait()
-    dHa[1] += mm(LX[2, :, :half], half_panel(dGb, 0), NT) + mm(LX[2, :, half:], half_panel(dGb, 1), NT)
+    back_in(2, dGb)
     px.wait()
 
     def back_one(m, _):

time: 308 us -> 302 us (0.981); the launches traced: 302 us -> 302 us
  no operation moved by 1% of the time
where the time goes in v2:
time: 302 us
  Pallas kernels  274 us (91%)
  local copies, waits for them, and re-layouts  19.3 us (6%)
  other arithmetic  7.17 us (2%)
    pallas_call x1, Pallas kernels, block_call(): pl.pallas_call(functools.partial(block_body, parts, nz), name='block', ou...  274 us

profile of v2, /device:TPU:0, one launch (start us, length us, event | category | flops | bytes accessed | tf_op | source)
XLA Modules:
  0.0 301.9 jit_solution(1329550210987660433)
XLA Ops:
  0.7 0.1 pad.28.clone
  0.7 0.7 convert.17
  1.5 0.7 convert_bitcast_fusion
  2.2 0.1 copy.102
  2.3 0.6 pad.12.b4
  2.9 0.7 copy.134
  3.6 0.1 concatenate.19
  3.7 0.1 compare_bitcast_fusion.1
  3.8 1.5 convert_element_type.34.b3
  5.3 0.2 copy.100
  5.5 0.2 copy.101
  5.7 0.1 add_add_fusion
  5.9 1.0 convert_element_type.33
  6.9 0.7 fusion
  7.6 0.7 pad_convert_fusion.masks
  8.4 0.9 reshape.66
  9.3 0.1 copy_bitcast_fusion.3
  9.4 0.2 copy_bitcast_fusion.2
  9.6 0.2 reshape.68
  9.8 0.2 reshape.67
  10.0 0.9 reshape.69
  10.9 0.1 copy_bitcast_fusion.1
  11.0 0.2 copy_bitcast_fusion
  11.2 0.2 reshape.71
  11.5 0.2 reshape.70
  11.7 0.9 pad_maximum_fusion.gus
  12.6 0.8 convert_element_type.37.ds
  13.4 274.5 %block.1 = (bf16[512,1024]{1,0:T(8,128)(2,1)}, bf16[512,1024]{1,0:T(8,128)(2,1)}, bf16[4,2,32,1152]{3,2,1,0:T(8,128)(2,1)}, f32[144,1024]{1,0:T(8,128)}, f32[32,...) custom-call(bf16[512,1024]{1,0:T(8,128)(2,1)} %bitcast.51, ...), custom_call_target="tpu_custom_call" | custom-call | tf_op jit(solution)/shard_map/block/pallas_call | solution.py:1062
  287.8 0.7 slice_bitcast_fusion.2
  288.6 0.7 slice_reduce_fusion
  289.3 0.1 slice.91
  289.3 0.7 copy.115
  290.0 1.1 slice_bitcast_fusion
  291.1 0.3 reshape.76
  291.4 0.2 reshape.77
  291.7 0.3 reshape.74
  292.1 0.2 reshape.75
  292.3 0.2 maximum_convert_fusion
  292.5 0.7 copy.109
  293.2 1.8 reshape.78
  295.0 0.2 maximum_convert_fusion.1
  295.2 0.7 copy.112
  295.9 1.8 reshape.79
  297.7 1.0 copy.140
  298.7 1.0 copy.141
  299.6 0.7 copy.142
  300.4 0.7 copy.143
  301.0 0.8 copy.144
  (30 shorter events, 0.4 us)
Async XLA Ops:
  0.6 7.7 %copy-start.2 = (f32[32,4608]{1,0:T(8,128)S(1)}, f32[32,4608]{1,0:T(8,128)}, u32[]{:S(2)}) copy-start(f32[32,4608]{1,0:T(8,128)} %param.18) | copy-start | bytes 1769476
  6.9 3.1 %copy-start.3 = (f32[32,4608]{1,0:T(8,128)S(1)}, f32[32,4608]{1,0:T(8,128)}, u32[]{:S(2)}) copy-start(f32[32,4608]{1,0:T(8,128)} %param.19) | copy-start | bytes 1769476
  10.9 1.7 copy-start.4
  295.2 2.5 copy-start.1
  295.9 2.7 copy-start
  297.7 2.0 copy-start.6
  297.7 2.7 copy-start.7
  298.7 2.4 copy-start.5

commit v3 on v2

--- a/solution.py
+++ b/solution.py
@@ -813,7 +813,7 @@
                 x_send1(0, 0, dHa[1])
                 for e in (1, 2, 0):
                     x_sent(0, e)
-                advance((0, 0), (0, 0), (0, 0), (0, 1))
+                advance((0, 0), (0, 0), (0, 1))
         cg[k].drain()
         before = len(cp.pending)
         grads(k)
@@ -1281,13 +1281,13 @@
 
 
 def join_columns(g, parts, ny, nz):
-    rows = g.shape[1]
+    rows = g.shape[2]
     pieces, start, npos = [], 0, ny * nz
     for size in parts:
-        piece = g[:, :, npos * start : npos * (start + size)].reshape(TP, rows, ny, nz, size)
-        pieces.append(piece.transpose(1, 2, 0, 3, 4))
+        piece = g[..., npos * start : npos * (start + size)].reshape(TP, 2, rows, ny, nz, size)
+        pieces.append(piece.transpose(1, 2, 3, 0, 4, 5))
         start += size
-    return jnp.concatenate(pieces, axis=-1).reshape(rows, -1).astype(F32)
+    return jnp.concatenate(pieces, axis=-1).reshape(2, rows, -1)
 
 
 def fast_device(
@@ -1327,8 +1327,7 @@
         tokens.reshape(rows, width), cotangent.reshape(rows, width), masks, blocks, gus,
         down_weight.astype(BF), parts, nz, 0
     )
-    g_gate = join_columns(gu[:, 0], parts, ny, nz)
-    g_up = join_columns(gu[:, 1], parts, ny, nz)
+    g_gate, g_up = (g.astype(F32) for g in join_columns(gu, parts, ny, nz))
     g_small = g_small[:, : taps + 2].T
     shape = tokens.shape
     return (

time: 302 us -> 301 us (level)
  no operation moved by 1% of the time
where the time goes in v3:
time: 301 us; the launch traced here: 300 us
  Pallas kernels  272 us (90%)
  local copies, waits for them, and re-layouts  20.1 us (7%)
  other arithmetic  7.16 us (2%)
    pallas_call x1, Pallas kernels, block_call(): pl.pallas_call(functools.partial(block_body, parts, nz), name='block', ou...  272 us

profile of v3, /device:TPU:0, one launch (start us, length us, event | category | flops | bytes accessed | tf_op | source)
XLA Modules:
  0.0 300.2 jit_solution(9360217561195534301)
XLA Ops:
  0.7 0.1 pad.26.clone
  0.7 0.7 convert.17
  1.5 0.7 convert_bitcast_fusion
  2.2 0.1 copy.100
  2.3 0.6 pad.12.b4
  2.9 0.7 copy.126
  3.6 0.1 concatenate.16
  3.7 0.1 compare_bitcast_fusion.1
  3.8 1.5 convert_element_type.34.b3
  5.3 0.2 copy.98
  5.5 0.2 copy.99
  5.7 0.1 add_add_fusion
  5.9 1.0 convert_element_type.33
  6.9 0.7 fusion.3
  7.6 0.7 pad_convert_fusion.masks
  8.4 0.9 reshape.63
  9.3 0.1 copy_bitcast_fusion.5
  9.4 0.2 copy_bitcast_fusion.4
  9.6 0.2 reshape.65
  9.8 0.2 reshape.64
  10.0 0.9 reshape.66
  10.9 0.1 copy_bitcast_fusion.3
  11.0 0.2 copy_bitcast_fusion.2
  11.2 0.2 reshape.68
  11.5 0.2 reshape.67
  11.7 0.9 pad_maximum_fusion.gus
  12.6 0.8 convert_element_type.37.ds
  13.4 272.1 %block.1 = (bf16[512,1024]{1,0:T(8,128)(2,1)}, bf16[512,1024]{1,0:T(8,128)(2,1)}, bf16[4,2,32,1152]{3,2,1,0:T(8,128)(2,1)}, f32[144,1024]{1,0:T(8,128)}, f32[32,...) custom-call(bf16[512,1024]{1,0:T(8,128)(2,1)} %bitcast.47, ...), custom_call_target="tpu_custom_call" | custom-call | tf_op jit(solution)/shard_map/block/pallas_call | solution.py:1062
  285.4 0.7 slice_bitcast_fusion
  286.1 0.7 slice_reduce_fusion
  286.8 0.1 slice.77
  286.9 0.7 copy.111
  287.6 1.0 slice.68
  288.5 1.0 slice.67
  289.6 0.6 reshape.71
  290.1 0.1 copy.125
  290.2 0.3 reshape.72
  290.5 0.1 copy.124
  290.6 0.5 fusion.2
  291.1 0.7 copy.108
  291.8 1.8 reshape.74
  293.6 0.7 copy.107
  294.2 1.8 reshape.73
  296.0 1.0 copy.132
  297.0 1.0 copy.133
  298.0 0.7 copy.134
  298.7 0.7 copy.135
  299.4 0.8 copy.136
  (22 shorter events, 0.2 us)
Async XLA Ops:
  0.6 7.7 %copy-start.2 = (f32[32,4608]{1,0:T(8,128)S(1)}, f32[32,4608]{1,0:T(8,128)}, u32[]{:S(2)}) copy-start(f32[32,4608]{1,0:T(8,128)} %param.18) | copy-start | bytes 1769476
  6.9 3.1 %copy-start.3 = (f32[32,4608]{1,0:T(8,128)S(1)}, f32[32,4608]{1,0:T(8,128)}, u32[]{:S(2)}) copy-start(f32[32,4608]{1,0:T(8,128)} %param.19) | copy-start | bytes 1769476
  10.9 1.7 copy-start.4
  293.5 2.4 copy-start.1
  294.2 2.7 copy-start
  296.0 2.0 copy-start.6
  296.0 2.7 copy-start.7
  297.0 2.4 copy-start.5
